TPU v7x, 32 devices: a whole 2x2x4 slice. The times are simulated.
32 devices in a mesh: tok: 2 (over core), head: 4 (over y, x), exp: 4 (over z).
Axes of the slice: x: 2, y: 2, z: 4, core: 2. Of those that a mesh axis runs over, the one named last changes fastest.
Arguments:
- context: bfloat16 [4, 64, 4096], P('exp', 'tok', 'head'), may hold values from -6 to 6
- out_proj: bfloat16 [4096, 4096], P('head', 'exp'), may hold values from -0.125 to 0.125
- stream: float32 [4, 64, 4096], P('exp', 'tok', 'head'), may hold values from -75 to 75
- norm_gain: float32 [4096], replicated, may hold values from 0.1 to 1.9
- expert_ids: int32 [4, 64, 8], P('exp', 'tok'), may hold values from 0 to 31, as said below
- slot_ids: int32 [4, 64, 8], P('exp', 'tok'), may hold values from -1 to 11, as said below
- gate_probs: float32 [4, 64, 8], P('exp', 'tok'), may hold values from 0.02 to 0.3
- w_gate: bfloat16 [32, 3072, 4096], P(('tok', 'exp'), 'head'), may hold values from -0.09375 to 0.09375
- w_up: bfloat16 [32, 3072, 4096], P(('tok', 'exp'), 'head'), may hold values from -0.09375 to 0.09375
- w_down: bfloat16 [32, 3072, 4096], P(('tok', 'exp'), 'head'), may hold values from -0.15625 to 0.15625
Outputs:
- mixed: float32 [4, 64, 4096], P('exp', 'tok', 'head')
Inputs may be any that keep to these rules, and one draw needn't show every extreme that they name: `expert_ids`: each token names 8 different experts. `slot_ids`: within a block of 32 consecutive tokens of one image, the choices of one expert take slots 0, 1, 2, ... in token order until its 12 slots are full, later ones get -1; in every block some expert fills all 12 slots.
All inputs are finite; a program needn't handle non-finite values.
Results may differ from a plain program's by a relative error of at most 0.0034.
Values may be sent and summed in bfloat16 or wider, within the bound.
A program may use at most 128 MiB of HBM per device.

v0:
```python
import jax
import jax.numpy as jnp
from jax import lax
from jax.sharding import PartitionSpec as P

EXPERTS = 32
TOP = 8
CAP = 12
eps_value = 1e-05


def on_device(
    context, out_proj, stream, norm_gain, expert_ids, slot_ids, gate_probs, w_gate, w_up, w_down
):
    local_context = context[0]
    own_stream = stream[0]
    col_width = own_stream.shape[1]
    col_start = lax.axis_index("head") * col_width
    partial_value = jnp.dot(
        local_context,
        lax.all_gather(out_proj, "exp", axis=1, tiled=True),
        preferred_element_type=jnp.float32,
    )
    own_sum = lax.dynamic_slice_in_dim(partial_value, col_start, col_width, 1) + own_stream
    partial_value = lax.dynamic_update_slice_in_dim(partial_value, own_sum, col_start, 1)
    resid_full = lax.psum(partial_value, "head")
    resid_own = lax.dynamic_slice_in_dim(resid_full, col_start, col_width, 1)
    mean_sq = jnp.mean(resid_full * resid_full, axis=1, keepdims=True)
    gain_own = lax.dynamic_slice_in_dim(norm_gain, col_start, col_width, 0)
    normed_own = (resid_own * lax.rsqrt(mean_sq + eps_value) * gain_own).astype(jnp.bfloat16)
    choice_ids = expert_ids[0]
    choice_slots = slot_ids[0]
    weights = gate_probs[0]
    spill_slot = EXPERTS * CAP
    target = jnp.where(choice_slots >= 0, choice_ids * CAP + choice_slots, spill_slot)
    outgoing = (
        jnp.zeros((spill_slot + 1, col_width), jnp.bfloat16)
        .at[target.reshape(-1)]
        .set(jnp.repeat(normed_own, TOP, axis=0))
    )
    outgoing = outgoing[:spill_slot].reshape(EXPERTS, CAP, col_width)
    tok_count = lax.axis_size("tok")
    groups = tok_count * lax.axis_size("exp")
    local_experts = w_gate.shape[0]
    arrived = lax.all_to_all(outgoing, ("tok", "exp"), split_axis=0, concat_axis=0, tiled=True)
    arrived = arrived.reshape(groups, local_experts, CAP, col_width)
    piece = lax.all_gather(arrived, "head", axis=3, tiled=True)
    gate_more = jnp.einsum("slcd,lhd->slch", piece, w_gate, preferred_element_type=jnp.float32)
    up_more = jnp.einsum("slcd,lhd->slch", piece, w_up, preferred_element_type=jnp.float32)
    hidden = (jax.nn.silu(gate_more) * up_more).astype(jnp.bfloat16)
    produced = jnp.einsum(
        "slch,lhd->slcd", hidden, w_down, preferred_element_type=jnp.float32
    ).astype(jnp.bfloat16)
    widened = lax.optimization_barrier(produced).astype(jnp.float32)
    summed = lax.psum_scatter(
        widened.astype(jnp.bfloat16), "head", scatter_dimension=3, tiled=True
    ).astype(jnp.float32)
    returned_share = lax.all_to_all(
        summed.reshape(EXPERTS, CAP, col_width).astype(jnp.bfloat16),
        ("tok", "exp"),
        split_axis=0,
        concat_axis=0,
        tiled=True,
    ).astype(jnp.float32)
    lookup_share = jnp.concatenate(
        [returned_share.reshape(spill_slot, col_width), jnp.zeros((1, col_width), jnp.float32)],
        axis=0,
    )
    picked_share = lookup_share[target]
    expert_own = jnp.sum(picked_share * weights[:, :, None], axis=1)
    return (resid_own + expert_own)[None]


def solution(mesh):
    in_specs = (
        P("exp", "tok", "head"),
        P("head", "exp"),
        P("exp", "tok", "head"),
        P(),
        P("exp", "tok", None),
        P("exp", "tok", None),
        P("exp", "tok", None),
        P(("tok", "exp"), "head", None),
        P(("tok", "exp"), "head", None),
        P(("tok", "exp"), "head", None),
    )
    out_specs = P("exp", "tok", "head")
    return jax.shard_map(
        on_device, mesh=mesh, in_specs=in_specs, out_specs=out_specs, check_vma=False
    )
```

profile of v0, /device:TPU:0, one launch (start us, length us, event | category | flops | bytes accessed | tf_op | source)
XLA Modules:
  0.0 433.1 jit_solution(15233698592753137792)
XLA Ops:
  6.5 0.7 all-gather.3.cloned.1.call-update
  7.4 153.9 %all-gather.3.cloned.1.call-done = bf16[1024,4096]{1,0:T(8,128)(2,1)} async-done(((bf16[1024,1024]{1,0:T(8,128)(2,1)}), bf16[1024,4096]{1,0:T(8,128)(2,1)}) %all-gather.3.cloned.1.call-update) | async-done | bytes 8388624 | tf_op jit(solution)/shard_map/all_gather | solution.py:21
  161.3 4.9 %fusion.24 = f32[32,4096]{1,0:T(8,128)S(1)} fusion(bf16[1024,4096]{1,0:T(8,128)(2,1)} %all-gather.3.cloned.1.call-done, bf16[1,32,1024]{2,1,0:T(8,128)(2,1)S(1)} %copy-done), kind=kOutput, calls=%fused_computation.29 | convolution fusion | flops 268435456 | bytes 8978432 | tf_op jit(solution)/shard_map/dot_general | solution.py:19
  166.2 0.8 copy-done.2
  167.1 0.0 all-gather.5.cloned.1.call-start
  167.1 0.1 copy.19
  167.2 0.1 select_n.53
  167.3 43.5 %all-reduce.3.cloned.1.call-done = f32[32,4096]{1,0:T(8,128)} async-done(((f32[32,4096]{1,0:T(8,128)}), f32[32,4096]{1,0:T(8,128)}) %all-reduce.3.cloned.1.call-update) | async-done | bytes 524304 | tf_op jit(solution)/shard_map/psum | solution.py:26
  210.8 1.2 multiply_reduce_fusion
  212.0 1.0 multiply_convert_fusion
  213.0 1.9 scatter_custom_fusion
  214.9 0.1 slice.6
  214.9 0.2 reshape.125
  215.1 30.6 %all_to_all.10 = bf16[32,12,1024]{2,1,0:T(8,128)(2,1)S(1)} all-to-all(bf16[32,12,1024]{2,1,0:T(8,128)(2,1)S(1)} %reshape.125), channel_id=1, replica_groups=mesh['tok'=2,'head'=4,'exp'=4] {'tok','exp'}, dimensions={0} | all-to-all | bytes 1572864 | tf_op jit(solution)/shard_map/all_to_all | solution.py:45
  245.7 1.0 copy.21
  246.8 0.2 reduce-scatter.2.cloned.1.call-start
  247.0 50.0 %all-gather.5.cloned.1.call-done = bf16[8,4,12,4096]{3,2,0,1:T(8,128)(2,1)} async-done(((bf16[8,4,12,1024]{3,2,0,1:T(8,128)(2,1)}), bf16[8,4,12,4096]{3,2,0,1:T(8,128)(2,1)}) %all-gather.5.cloned.1.call-update) | async-done | bytes 3145744 | tf_op jit(solution)/shard_map/all_gather | solution.py:47
  297.0 13.4 %fusion.4 = f32[4,8,12,768]{3,2,1,0:T(8,128)S(1)} fusion(bf16[8,4,12,4096]{3,2,0,1:T(8,128)(2,1)} %all-gather.5.cloned.1.call-done, bf16[4,768,4096]{2,1,0:T(8,128)(2,1)} %param.17), kind=kOutput, calls=%fused_computation.6 | convolution fusion | flops 2415919104 | bytes 29491200 | tf_op jit(solution)/shard_map/slcd,lhd->slch/dot_general | solution.py:48
  310.4 13.5 %fusion.12 = bf16[8,4,12,768]{3,2,0,1:T(8,128)(2,1)S(1)} fusion(f32[4,8,12,768]{3,2,1,0:T(8,128)S(1)} %fusion.4, bf16[8,4,12,4096]{3,2,0,1:T(8,128)(2,1)} %all-gather.5.cloned.1.call-done, bf16[4,768,4096]{2,1,0:T(8,128)(2,1)} %param.18), kind=kOutput, calls=%fused_computation.11 | convolution fusion | flops 2417688576 | bytes 30081024 | tf_op jit(solution)/shard_map/slcd,lhd->slch/dot_general | solution.py:49
  323.9 13.6 %fusion.9 = bf16[8,4,12,4096]{3,2,0,1:T(8,128)(2,1)} fusion(bf16[8,4,12,768]{3,2,0,1:T(8,128)(2,1)S(1)} %fusion.12, bf16[4,768,4096]{2,1,0:T(8,128)(2,1)} %param.19), kind=kOutput, calls=%fused_computation.9 | convolution fusion | flops 2417491968 | bytes 28901376 | tf_op jit(solution)/shard_map/slch,lhd->slcd/dot_general | solution.py:51
  337.5 52.7 %reduce-scatter.2.cloned.1.call-done = bf16[8,4,12,1024]{3,2,0,1:T(8,128)(2,1)} async-done(((bf16[8,4,12,4096]{3,2,0,1:T(8,128)(2,1)}), bf16[8,4,12,1024]{3,2,0,1:T(8,128)(2,1)}) %reduce-scatter.2.cloned.1.call-update) | async-done | bytes 786448 | tf_op jit(solution)/shard_map/reduce_scatter | solution.py:55
  390.2 2.3 copy.31
  392.5 4.6 %all-to-all-start.1 = ((bf16[32,12,1024]{2,1,0:T(8,128)(2,1)}), bf16[32,12,1024]{2,1,0:T(8,128)(2,1)S(1)}, u32[]{:S(2)}, u32[]{:S(2)}) async-start(bf16[32,12,1024]{2,1,0:T(8,128)(2,1)} %bitcast.14), calls=%async_computation.2 | async-start | bytes 2097152 | tf_op jit(solution)/shard_map/all_to_all | solution.py:58
  397.1 0.1 copy.24
  397.2 0.1 reshape.130
  397.3 0.1 copy.25
  397.4 25.7 %all-to-all-done.1 = bf16[32,12,1024]{2,1,0:T(8,128)(2,1)S(1)} async-done(((bf16[32,12,1024]{2,1,0:T(8,128)(2,1)}), bf16[32,12,1024]{2,1,0:T(8,128)(2,1)S(1)}, u32[]{:S(2)}, u32[]{:S(2)}) %all-to-all-start.1) | async-done | bytes 786464 | tf_op jit(solution)/shard_map/all_to_all | solution.py:58
  423.1 0.2 reshape.127
  423.3 0.2 pad_convert_fusion
  423.5 1.1 gather_fusion
  424.6 0.4 fusion.18
  424.9 1.6 add_bitcast_fusion
  (25 shorter events, 0.2 us)
Async XLA Ops:
  6.5 154.7 %copy-start = (bf16[1,32,1024]{2,1,0:T(8,128)(2,1)S(1)}, bf16[1,32,1024]{2,1,0:T(8,128)(2,1)}, u32[]{:S(2)}) copy-start(bf16[1,32,1024]{2,1,0:T(8,128)(2,1)} %param.10) | copy-start | bytes 196612
  6.5 154.7 %all-gather.3.cloned.1.call-start = ((), (), s32[]{:S(2)}) async-start(), calls=%async_computation.3 | async-start | bytes 10485760 | tf_op jit(solution)/shard_map/all_gather | solution.py:21
  7.3 203.5 %all-reduce.3.cloned.1.call-start = ((), (), s32[]{:S(2)}) async-start(), calls=%async_computation.4 | async-start | bytes 1048576 | tf_op jit(solution)/shard_map/psum | solution.py:26
  7.3 158.9 %copy-start.3 = (f32[1,32,1024]{2,1,0:T(8,128)S(1)}, f32[1,32,1024]{2,1,0:T(8,128)}, u32[]{:S(2)}) copy-start(f32[1,32,1024]{2,1,0:T(8,128)} %param.12) | copy-start | bytes 393220
  7.3 159.8 %copy-start.5 = (s32[1,32,8]{1,2,0:T(8,128)S(1)}, s32[1,32,8]{1,2,0:T(8,128)}, u32[]{:S(2)}) copy-start(s32[1,32,8]{1,2,0:T(8,128)} %param.15) | copy-start | bytes 3076
  7.3 159.8 %copy-start.6 = (s32[1,32,8]{1,2,0:T(8,128)S(1)}, s32[1,32,8]{1,2,0:T(8,128)}, u32[]{:S(2)}) copy-start(s32[1,32,8]{1,2,0:T(8,128)} %param.14) | copy-start | bytes 3076
  7.3 204.6 %dynamic-slice-start = ((f32[4096]{0:T(1024)}, s32[]{:T(128)}), f32[1024]{0:T(1024)S(1)}, s32[]{:S(2)}) async-start(f32[4096]{0:T(1024)} %param.13, s32[]{:T(128)} %select_n.51), calls=%async_computation.7 | async-start | bytes 8704 | tf_op jit(solution)/shard_map/dynamic_slice | solution.py:29
  166.2 0.8 copy-start.2
  167.1 129.9 %all-gather.5.cloned.1.call-start = ((), (), s32[]{:S(2)}) async-start(), calls=%async_computation.5 | async-start | bytes 5242880 | tf_op jit(solution)/shard_map/all_gather | solution.py:47
  246.8 143.4 %reduce-scatter.2.cloned.1.call-start = ((), (), s32[]{:S(2)}) async-start(), calls=%async_computation.6 | async-start | bytes 5242880 | tf_op jit(solution)/shard_map/reduce_scatter | solution.py:55
  337.5 59.8 %copy-start.4 = (f32[1,32,8]{1,2,0:T(8,128)S(1)}, f32[1,32,8]{1,2,0:T(8,128)}, u32[]{:S(2)}) copy-start(f32[1,32,8]{1,2,0:T(8,128)} %param.16) | copy-start | bytes 3076
  392.5 30.6 %all-to-all-start.1 = ((bf16[32,12,1024]{2,1,0:T(8,128)(2,1)}), bf16[32,12,1024]{2,1,0:T(8,128)(2,1)S(1)}, u32[]{:S(2)}, u32[]{:S(2)}) async-start(bf16[32,12,1024]{2,1,0:T(8,128)(2,1)} %bitcast.14), calls=%async_computation.2 | async-start | bytes 2097152 | tf_op jit(solution)/shard_map/all_to_all | solution.py:58
  423.3 3.2 copy-start.1
Sparse Core Ops, SparseCore 0:
  8.9 152.3 all-gather.2
  167.2 43.5 all-reduce.2
  246.9 50.0 all-gather.4
  337.6 52.5 reduce-scatter.1
where the time goes:
time: 433 us
  waiting for transfers between devices  327 us (76%)
  matrix products  45.4 us (10%)
  blocking collectives  30.6 us (7%)
  between operations  13.3 us (3%)
  local copies, waits for them, and re-layouts  7.94 us (2%)
  starting transfers between devices  4.91 us (1%)
  other arithmetic  4.33 us (1%)
    all_gather x1, waiting for transfers between devices, on_device(): lax.all_gather(out_proj, 'exp', axis=1, tiled=True)  154 us
    reduce_scatter x1, waiting for transfers between devices, on_device(): lax.psum_scatter(widened.astype(jnp.bfloat16), 'head', scatter_dimension=...  52.7 us
    all_gather x1, waiting for transfers between devices, on_device(): piece = lax.all_gather(arrived, 'head', axis=3, tiled=True)  50 us
    psum x1, waiting for transfers between devices, on_device(): resid_full = lax.psum(partial_value, 'head')  43.5 us
    all_to_all x1, blocking collectives, on_device(): lax.all_to_all(outgoing, ('tok', 'exp'), split_axis=0, concat_axis=0, til...  30.6 us
    all_to_all x1, waiting for transfers between devices, on_device(): lax.all_to_all(summed.reshape(EXPERTS, CAP, col_width).astype(jnp.bfloat1...  25.7 us
    dot_general x1, matrix products, on_device(): jnp.einsum('slch,lhd->slcd', hidden, w_down, preferred_element_type=jnp.f...  13.6 us
    dot_general x1, matrix products, on_device(): jnp.einsum('slcd,lhd->slch', piece, w_up, preferred_element_type=jnp.floa...  13.5 us
  transfers between devices with their start and end apart: 5, of which 5 were waited for; matrix products, arithmetic and copies ran while one was open for 0% of the time, Pallas kernels for 0%

commit v1 on v0

--- a/solution.py
+++ b/solution.py
@@ -18,7 +18,7 @@
     col_start = lax.axis_index("head") * col_width
     partial_value = jnp.dot(
         local_context,
-        lax.all_gather(out_proj, "exp", axis=1, tiled=True),
+        jnp.concatenate(lax.all_gather(out_proj, "exp"), axis=1),
         preferred_element_type=jnp.float32,
     )
     own_sum = lax.dynamic_slice_in_dim(partial_value, col_start, col_width, 1) + own_stream

time: 433 us -> 446 us (1.030)
  local copies, waits for them, and re-layouts: 7.94 us -> 19.4 us
    reshape x0 -> x1, local copies, waits for them, and re-layouts: none -> 11.4 us  [on_device(): jnp.concatenate(lax.all_gather(out_proj, 'exp'), axis=1)]
where the time goes in v1:
time: 446 us
  waiting for transfers between devices  327 us (73%)
  matrix products  46.5 us (10%)
  blocking collectives  30.6 us (7%)
  local copies, waits for them, and re-layouts  19.4 us (4%)
  between operations  13.3 us (3%)
  starting transfers between devices  4.91 us (1%)
    all_gather x1, waiting for transfers between devices, on_device(): lax.all_gather(out_proj, 'exp')  154 us
    reduce_scatter x1, waiting for transfers between devices, on_device(): lax.psum_scatter(widened.astype(jnp.bfloat16), 'head', scatter_dimension=...  52.8 us
    all_gather x1, waiting for transfers between devices, on_device(): piece = lax.all_gather(arrived, 'head', axis=3, tiled=True)  50 us
    psum x1, waiting for transfers between devices, on_device(): resid_full = lax.psum(partial_value, 'head')  43.5 us
    all_to_all x1, blocking collectives, on_device(): lax.all_to_all(outgoing, ('tok', 'exp'), split_axis=0, concat_axis=0, til...  30.6 us
    all_to_all x1, waiting for transfers between devices, on_device(): lax.all_to_all(summed.reshape(EXPERTS, CAP, col_width).astype(jnp.bfloat1...  25.7 us
    dot_general x1, matrix products, on_device(): jnp.einsum('slch,lhd->slcd', hidden, w_down, preferred_element_type=jnp.f...  13.6 us
    dot_general x1, matrix products, on_device(): jnp.einsum('slcd,lhd->slch', piece, w_up, preferred_element_type=jnp.floa...  13.5 us
  transfers between devices with their start and end apart: 5, of which 5 were waited for; matrix products, arithmetic and copies ran while one was open for 0% of the time, Pallas kernels for 0%

profile of v1, /device:TPU:0, one launch (start us, length us, event | category | flops | bytes accessed | tf_op | source)
XLA Modules:
  0.0 445.6 jit_solution(1624429252074337224)
XLA Ops:
  6.5 0.7 all-gather.6.cloned.1.call-update
  7.3 154.0 %all-gather.6.cloned.1.call-done = bf16[4096,1024]{1,0:T(8,128)(2,1)} async-done(((bf16[1024,1024]{1,0:T(8,128)(2,1)}), bf16[4096,1024]{1,0:T(8,128)(2,1)}) %all-gather.6.cloned.1.call-update) | async-done | bytes 8388624 | tf_op jit(solution)/shard_map/all_gather | solution.py:21
  161.3 11.4 %copy.27 = bf16[1024,4,1024]{0,2,1:T(8,128)(2,1)} copy(bf16[1024,4,1024]{2,0,1:T(8,128)(2,1)} %bitcast.74) | data formatting | bytes 16777216 | tf_op jit(solution)/shard_map/reshape | solution.py:21
  172.7 6.0 %fusion.24 = f32[32,4096]{1,0:T(8,128)S(1)} fusion(bf16[1024,4096]{0,1:T(8,128)(2,1)} %bitcast.73, bf16[1,32,1024]{2,1,0:T(8,128)(2,1)S(1)} %copy-done), kind=kOutput, calls=%fused_computation.29 | convolution fusion | flops 268435456 | bytes 8978432 | tf_op jit(solution)/shard_map/dot_general | solution.py:19
  178.8 0.8 copy-done.2
  179.7 0.1 copy.28
  179.8 0.1 select_n.53
  179.9 43.5 %all-reduce.3.cloned.1.call-done = f32[32,4096]{1,0:T(8,128)} async-done(((f32[32,4096]{1,0:T(8,128)}), f32[32,4096]{1,0:T(8,128)}) %all-reduce.3.cloned.1.call-update) | async-done | bytes 524304 | tf_op jit(solution)/shard_map/psum | solution.py:26
  223.3 1.2 multiply_reduce_fusion
  224.5 1.0 multiply_convert_fusion
  225.5 1.9 scatter_custom_fusion
  227.4 0.1 slice.6
  227.5 0.2 reshape.133
  227.7 30.6 %all_to_all.10 = bf16[32,12,1024]{2,1,0:T(8,128)(2,1)S(1)} all-to-all(bf16[32,12,1024]{2,1,0:T(8,128)(2,1)S(1)} %reshape.133), channel_id=1, replica_groups=mesh['tok'=2,'head'=4,'exp'=4] {'tok','exp'}, dimensions={0} | all-to-all | bytes 1572864 | tf_op jit(solution)/shard_map/all_to_all | solution.py:45
  258.3 1.0 copy.30
  259.3 0.2 reduce-scatter.2.cloned.1.call-start
  259.6 50.0 %all-gather.4.cloned.1.call-done = bf16[8,4,12,4096]{3,2,0,1:T(8,128)(2,1)} async-done(((bf16[8,4,12,1024]{3,2,0,1:T(8,128)(2,1)}), bf16[8,4,12,4096]{3,2,0,1:T(8,128)(2,1)}) %all-gather.4.cloned.1.call-update) | async-done | bytes 3145744 | tf_op jit(solution)/shard_map/all_gather | solution.py:47
  309.5 13.4 %fusion.4 = f32[4,8,12,768]{3,2,1,0:T(8,128)S(1)} fusion(bf16[8,4,12,4096]{3,2,0,1:T(8,128)(2,1)} %all-gather.4.cloned.1.call-done, bf16[4,768,4096]{2,1,0:T(8,128)(2,1)} %param.17), kind=kOutput, calls=%fused_computation.6 | convolution fusion | flops 2415919104 | bytes 29491200 | tf_op jit(solution)/shard_map/slcd,lhd->slch/dot_general | solution.py:48
  323.0 13.5 %fusion.12 = bf16[8,4,12,768]{3,2,0,1:T(8,128)(2,1)S(1)} fusion(f32[4,8,12,768]{3,2,1,0:T(8,128)S(1)} %fusion.4, bf16[8,4,12,4096]{3,2,0,1:T(8,128)(2,1)} %all-gather.4.cloned.1.call-done, bf16[4,768,4096]{2,1,0:T(8,128)(2,1)} %param.18), kind=kOutput, calls=%fused_computation.11 | convolution fusion | flops 2417688576 | bytes 30081024 | tf_op jit(solution)/shard_map/slcd,lhd->slch/dot_general | solution.py:49
  336.5 13.6 %fusion.9 = bf16[8,4,12,4096]{3,2,0,1:T(8,128)(2,1)} fusion(bf16[8,4,12,768]{3,2,0,1:T(8,128)(2,1)S(1)} %fusion.12, bf16[4,768,4096]{2,1,0:T(8,128)(2,1)} %param.19), kind=kOutput, calls=%fused_computation.9 | convolution fusion | flops 2417491968 | bytes 28901376 | tf_op jit(solution)/shard_map/slch,lhd->slcd/dot_general | solution.py:51
  350.0 52.8 %reduce-scatter.2.cloned.1.call-done = bf16[8,4,12,1024]{3,2,0,1:T(8,128)(2,1)} async-done(((bf16[8,4,12,4096]{3,2,0,1:T(8,128)(2,1)}), bf16[8,4,12,1024]{3,2,0,1:T(8,128)(2,1)}) %reduce-scatter.2.cloned.1.call-update) | async-done | bytes 786448 | tf_op jit(solution)/shard_map/reduce_scatter | solution.py:55
  402.8 2.3 copy.40
  405.1 4.6 %all-to-all-start.1 = ((bf16[32,12,1024]{2,1,0:T(8,128)(2,1)}), bf16[32,12,1024]{2,1,0:T(8,128)(2,1)S(1)}, u32[]{:S(2)}, u32[]{:S(2)}) async-start(bf16[32,12,1024]{2,1,0:T(8,128)(2,1)} %bitcast.17), calls=%async_computation.2 | async-start | bytes 2097152 | tf_op jit(solution)/shard_map/all_to_all | solution.py:58
  409.7 0.1 copy.33
  409.8 0.1 reshape.138
  409.9 0.1 copy.34
  410.0 25.7 %all-to-all-done.1 = bf16[32,12,1024]{2,1,0:T(8,128)(2,1)S(1)} async-done(((bf16[32,12,1024]{2,1,0:T(8,128)(2,1)}), bf16[32,12,1024]{2,1,0:T(8,128)(2,1)S(1)}, u32[]{:S(2)}, u32[]{:S(2)}) %all-to-all-start.1) | async-done | bytes 786464 | tf_op jit(solution)/shard_map/all_to_all | solution.py:58
  435.7 0.2 reshape.135
  435.9 0.2 pad_convert_fusion
  436.1 1.1 gather_fusion
  437.1 0.4 fusion.18
  437.5 1.6 add_bitcast_fusion
  (26 shorter events, 0.2 us)
Async XLA Ops:
  6.5 166.2 %copy-start = (bf16[1,32,1024]{2,1,0:T(8,128)(2,1)S(1)}, bf16[1,32,1024]{2,1,0:T(8,128)(2,1)}, u32[]{:S(2)}) copy-start(bf16[1,32,1024]{2,1,0:T(8,128)(2,1)} %param.10) | copy-start | bytes 196612
  6.5 154.7 %all-gather.6.cloned.1.call-start = ((), (), s32[]{:S(2)}) async-start(), calls=%async_computation.6 | async-start | bytes 10485760 | tf_op jit(solution)/shard_map/all_gather | solution.py:21
  7.3 216.1 %all-reduce.3.cloned.1.call-start = ((), (), s32[]{:S(2)}) async-start(), calls=%async_computation.3 | async-start | bytes 1048576 | tf_op jit(solution)/shard_map/psum | solution.py:26
  172.7 6.0 %copy-start.3 = (f32[1,32,1024]{2,1,0:T(8,128)S(1)}, f32[1,32,1024]{2,1,0:T(8,128)}, u32[]{:S(2)}) copy-start(f32[1,32,1024]{2,1,0:T(8,128)} %param.12) | copy-start | bytes 393220
  172.7 7.0 %copy-start.5 = (s32[1,32,8]{1,2,0:T(8,128)S(1)}, s32[1,32,8]{1,2,0:T(8,128)}, u32[]{:S(2)}) copy-start(s32[1,32,8]{1,2,0:T(8,128)} %param.15) | copy-start | bytes 3076
  172.7 7.0 %copy-start.6 = (s32[1,32,8]{1,2,0:T(8,128)S(1)}, s32[1,32,8]{1,2,0:T(8,128)}, u32[]{:S(2)}) copy-start(s32[1,32,8]{1,2,0:T(8,128)} %param.14) | copy-start | bytes 3076
  172.7 51.8 %dynamic-slice-start = ((f32[4096]{0:T(1024)}, s32[]{:T(128)}), f32[1024]{0:T(1024)S(1)}, s32[]{:S(2)}) async-start(f32[4096]{0:T(1024)} %param.13, s32[]{:T(128)} %select_n.51), calls=%async_computation.7 | async-start | bytes 8704 | tf_op jit(solution)/shard_map/dynamic_slice | solution.py:29
  178.8 0.8 copy-start.2
  179.6 129.9 %all-gather.4.cloned.1.call-start = ((), (), s32[]{:S(2)}) async-start(), calls=%async_computation.4 | async-start | bytes 5242880 | tf_op jit(solution)/shard_map/all_gather | solution.py:47
  259.3 143.5 %reduce-scatter.2.cloned.1.call-start = ((), (), s32[]{:S(2)}) async-start(), calls=%async_computation.5 | async-start | bytes 5242880 | tf_op jit(solution)/shard_map/reduce_scatter | solution.py:55
  350.0 59.9 %copy-start.4 = (f32[1,32,8]{1,2,0:T(8,128)S(1)}, f32[1,32,8]{1,2,0:T(8,128)}, u32[]{:S(2)}) copy-start(f32[1,32,8]{1,2,0:T(8,128)} %param.16) | copy-start | bytes 3076
  405.1 30.6 %all-to-all-start.1 = ((bf16[32,12,1024]{2,1,0:T(8,128)(2,1)}), bf16[32,12,1024]{2,1,0:T(8,128)(2,1)S(1)}, u32[]{:S(2)}, u32[]{:S(2)}) async-start(bf16[32,12,1024]{2,1,0:T(8,128)(2,1)} %bitcast.17), calls=%async_computation.2 | async-start | bytes 2097152 | tf_op jit(solution)/shard_map/all_to_all | solution.py:58
  435.9 3.2 copy-start.1
Sparse Core Ops, SparseCore 0:
  8.9 152.3 all-gather.5
  179.7 43.5 all-reduce.2
  259.5 50.0 all-gather.3
  350.2 52.5 reduce-scatter.1
